TPU v7x, 128 devices: a whole 4x4x4 slice. The times are simulated.
128 devices in a mesh: seg: 16 (over y, z), col: 8 (over x, core).
Axes of the slice: x: 4, y: 4, z: 4, core: 2. Of those that a mesh axis runs over, the one named last changes fastest.
Arguments:
- model_mixing: float32 [32, 384, 384], P('seg', 'col'), may hold values from -0.07654656 to 0.07654656
- retention: float32 [32, 384], P('seg'), may hold values from 0.5 to 0.95
- forcing: float32 [32, 384], P('seg'), may hold values from -1.2 to 1.2
- observations: float32 [32, 1024], P('seg'), may hold values from -6 to 6
- model_noise: float32 [32, 384], P('seg'), may hold values from 0.01 to 0.1
- obs_noise: float32 [1024], replicated, may hold values from 0.5 to 2
- gain: float32 [384, 1024], replicated, may hold values from -0.01875 to 0.01875
- obs_operator_t: float32 [384, 1024], P('col'), may hold values from -0.30618623 to 0.30618623
- prior_mean: float32 [384], replicated, may hold values from -6 to 6
- prior_factor: float32 [384, 384], replicated, may hold values from -0.3125 to 0.3125
Outputs:
- means: float32 [32, 384], P('seg')
- covariances: float32 [32, 384, 384], P('seg', 'col')
All inputs are finite; a program needn't handle non-finite values.
Results may differ from a plain program's by a relative error of at most 0.00019.
Values sent between devices are 32-bit elements; how exact they have to be, the bound alone decides.
A program may use at most 64 MiB of HBM per device.

v0:
```python
import functools

import jax
import jax.numpy as jnp
from jax import lax
from jax.experimental import pallas as pl
from jax.experimental.pallas import tpu as pltpu
from jax.sharding import Mesh
from jax.sharding import PartitionSpec as P

MESH = pl.DeviceIdType.MESH
F32 = jnp.float32
BF16 = jnp.bfloat16
SEG = ("y", "z")
COL = ("x", "c")
N = 384
NOBS = 1024
W = 48
CR = 24
PER_CLASS = 36


def split(value):
    high = value.astype(BF16)
    low = (value - high.astype(F32)).astype(BF16)
    return high, low


def dot(left, right, transposed):
    dims = (((1,), (1 if transposed else 0,)), ((), ()))
    return lax.dot_general(left, right, dims, preferred_element_type=F32)


def product(left, right_high, right_low, transposed=False):
    high, low = split(left)
    rows = left.shape[0]
    both = dot(jnp.concatenate([high, low], 0), right_high, transposed)
    return both[:rows] + (both[rows:] + dot(high, right_low, transposed))


def put_split(high_ref, low_ref, index, value):
    high, low = split(value)
    high_ref[index] = high
    low_ref[index] = low


def turn(position, by):
    return lax.rem(position + (by % 4), 4)


class PlaneGather:
    def __init__(self, unit, rows, core, first, second, to_first, to_second, partner, send, recv, base, sent):
        self.unit, self.rows, self.core = unit, rows, core
        self.f = [turn(first, d) for d in (0, -1, 1, 2)]
        self.s = [turn(second, d) for d in (0, -1, 1, 2)]
        self.to_first, self.to_second, self.partner = to_first, to_second, partner
        self.send, self.recv, self.base, self.sent = send, recv, base, sent

    def at(self, kf, ks, half=None, core=None):
        ref = self.unit(self.core if core is None else core, self.f[kf], self.s[ks])
        if half is None:
            return ref
        middle = self.rows // 2
        return ref.at[pl.ds(half * middle, middle)]

    def start(self, index, source, target, device):
        copy = pltpu.make_async_remote_copy(
            src_ref=source,
            dst_ref=target,
            send_sem=self.send.at[self.base + index],
            recv_sem=self.recv.at[self.base + index],
            device_id=device,
            device_id_type=MESH,
        )
        copy.start()
        self.sent.append(copy)

    def arrive(self, index, slot):
        pltpu.make_async_remote_copy(
            src_ref=slot,
            dst_ref=slot,
            send_sem=self.send.at[self.base + index],
            recv_sem=self.recv.at[self.base + index],
            device_id=self.partner,
            device_id_type=MESH,
        ).wait_recv()

    def first_own(self, source):
        for way in (0, 1):
            self.start(way, source, self.at(0, 0), self.to_first[way])

    def share(self, kf, ks, source=None):
        slot = self.at(kf, ks)
        self.start(20 + 4 * ks + kf, slot if source is None else source, slot, self.partner)

    def shared(self, kf, ks):
        self.arrive(20 + 4 * ks + kf, self.at(kf, ks, core=1 - self.core))

    def second(self, kf, source=None):
        slot = self.at(kf, 0)
        for way in (0, 1):
            self.start(4 + 2 * kf + way, slot if source is None else source, slot, self.to_second[way])

    def first_near(self):
        for way in (0, 1):
            self.arrive(way, self.at(1 + way, 0))
            part = self.at(1 + way, 0, half=way)
            self.start(2 + way, part, part, self.to_first[way])
            self.second(1 + way)
            self.share(1 + way, 0)

    def first_far(self):
        for way in (0, 1):
            self.arrive(2 + way, self.at(3, 0, half=way))
        self.second(3)
        self.share(3, 0)

    def second_near(self, kf):
        for way in (0, 1):
            self.arrive(4 + 2 * kf + way, self.at(kf, 1 + way))
            part = self.at(kf, 1 + way, half=way)
            self.start(12 + 2 * kf + way, part, part, self.to_second[way])
            self.share(kf, 1 + way)

    def second_far(self, kf):
        for way in (0, 1):
            self.arrive(12 + 2 * kf + way, self.at(kf, 3, half=way))
        self.share(kf, 3)


def kernel(
    mixing, retention, forcing, observations, model_noise, obs_noise, gain, obs_t, prior_mean, prior_factor,
    means, covariances,
    ga, gb, cg, ea, eb, ret4, forc4, obs4, noise4, ret8, forc16, obs16, noise8, on_v, gain_v, gain_h, gain_l,
    obs_v, pm_v, pf_v, ct_h, ct_l, fix_h, fix_l, p_h, p_l, b_h, b_l, off8, wc, gc, wf, gf, stage, stage_mean,
    near_mean, t1_h, t1_l, n1_h, n1_l, t2_h, t2_l, n2_h, n2_l, w0_s, v1_s, v2_s, xs,
    send1, recv1, send3, recv3, send_c, recv_c, send_s, recv_s, send_y, recv_y, local,
):
    y, z, x, c = (lax.axis_index(name) for name in ("y", "z", "x", "c"))
    partner = (y, z, x, 1 - c)
    x_to = [(y, z, turn(x, 1), c), (y, z, turn(x, -1), c)]
    z_to = [(y, turn(z, 1), x, c), (y, turn(z, -1), x, c)]
    x_far, z_far = (y, z, turn(x, 2), c), (y, turn(z, 2), x, c)
    y_to = [(turn(y, d), z, x, c) for d in (1, 2, 3)]
    sent = []

    own = {}
    for index, (name, source, target) in enumerate(
        (
            ("gain", gain, gain_v),
            ("obs_t", obs_t, obs_v),
            ("mix0", mixing.at[0], ga.at[c, z, x]),
            ("mix1", mixing.at[1], gb.at[c, x, z]),
            ("noise", obs_noise, on_v),
            ("ret", retention, ret4.at[z]),
            ("forc", forcing, forc4.at[z]),
            ("obs", observations, obs4.at[z]),
            ("mn", model_noise, noise4.at[z]),
            ("pm", prior_mean, pm_v),
            ("pf", prior_factor, pf_v),
        )
    ):
        own[name] = pltpu.make_async_copy(source, target, local.at[index])
        own[name].start()

    ea[c, z, x] = jnp.zeros((32, N), F32)
    eb[c, x, z] = jnp.zeros((32, N), F32)
    forc16[...] = jnp.zeros((16, N), F32)
    obs16[...] = jnp.zeros((16, NOBS), F32)

    barrier = pltpu.get_barrier_semaphore()
    friends = [partner] + x_to + [x_far] + z_to + [z_far] + y_to
    for friend in friends:
        pl.semaphore_signal(barrier, inc=1, device_id=friend, device_id_type=MESH)
    pl.semaphore_wait(barrier, len(friends))

    first = PlaneGather(lambda core, f, s: ga.at[core, s, f], W, c, x, z, x_to, z_to, partner, send1, recv1, 0, sent)
    other = PlaneGather(
        lambda core, f, s: gb.at[core, s, f], W, c, z, x, z_to, x_to, partner, send1, recv1, PER_CLASS, sent
    )
    first.first_own(mixing.at[0])
    other.first_own(mixing.at[1])
    first.second(0, mixing.at[0])
    first.share(0, 0, mixing.at[0])
    other.share(0, 0, mixing.at[1])

    small = []
    for array, (source, target) in enumerate(
        ((retention, ret4), (forcing, forc4), (observations, obs4), (model_noise, noise4))
    ):
        for d in (1, 2, 3):
            index = 3 * array + d - 1
            copy = pltpu.make_async_remote_copy(
                src_ref=source,
                dst_ref=target.at[z],
                send_sem=send_s.at[index],
                recv_sem=recv_s.at[index],
                device_id=(y, turn(z, d), x, c),
                device_id_type=MESH,
            )
            copy.start()
            sent.append(copy)
            slot = target.at[turn(z, -d)]
            small.append(
                pltpu.make_async_remote_copy(
                    src_ref=slot,
                    dst_ref=slot,
                    send_sem=send_s.at[index],
                    recv_sem=recv_s.at[index],
                    device_id=partner,
                    device_id_type=MESH,
                )
            )

    own["gain"].wait()
    own["obs_t"].wait()
    own["noise"].wait()
    put_split(gain_h, gain_l, ..., gain_v[...])
    rows_of = lax.broadcasted_iota(jnp.int32, (W, N), 0)
    cols_of = lax.broadcasted_iota(jnp.int32, (W, N), 1)
    start_row = x * 96 + c * W
    eye_rows = (rows_of + start_row == cols_of).astype(F32)
    cg[c, x] = eye_rows - product(obs_v[...], gain_h[...], gain_l[...], True)

    def fixed(part):
        rows = pl.ds(part * 128, 128)
        value = product(gain_v[rows, :] * on_v[...], gain_h[...], gain_l[...], True)
        put_split(fix_h, fix_l, rows, value)

    def send_gain(index, slot, device):
        copy = pltpu.make_async_remote_copy(
            src_ref=slot,
            dst_ref=slot,
            send_sem=send_c.at[index],
            recv_sem=recv_c.at[index],
            device_id=device,
            device_id_type=MESH,
        )
        copy.start()
        sent.append(copy)

    def recv_gain(index, slot):
        pltpu.make_async_remote_copy(
            src_ref=slot,
            dst_ref=slot,
            send_sem=send_c.at[index],
            recv_sem=recv_c.at[index],
            device_id=partner,
            device_id_type=MESH,
        ).wait_recv()

    for index, device in enumerate(x_to + [x_far, partner]):
        send_gain(index, cg.at[c, x], device)
    other.second(0, mixing.at[1])
    fixed(0)

    first.first_near()
    other.first_near()
    fixed(1)
    for index, d in enumerate((-1, 1, 2)):
        slot = cg.at[c, turn(x, d)]
        recv_gain(index, slot)
        send_gain(4 + index, slot, partner)
    first.second_near(0)
    other.second_near(0)
    fixed(2)
    first.first_far()
    other.first_far()

    for name in ("ret", "forc", "obs", "mn", "pm", "pf", "mix0", "mix1"):
        own[name].wait()
    for copy in small:
        copy.wait_recv()
    for place in range(4):
        for step in range(2):
            row = 2 * place + step
            ret8[pl.ds(row, 1), :] = ret4[place, pl.ds(step, 1), :]
            noise8[pl.ds(row, 1), :] = noise4[place, pl.ds(step, 1), :]
            forc16[pl.ds(row, 1), :] = forc4[place, pl.ds(step, 1), :]
            obs16[pl.ds(row, 1), :] = obs4[place, pl.ds(step, 1), :]

    recv_gain(3, cg.at[1 - c, x])
    for index, d in enumerate((-1, 1, 2)):
        recv_gain(4 + index, cg.at[1 - c, turn(x, d)])
    put_split(ct_h, ct_l, ..., jnp.concatenate([cg[core, place] for place in range(4) for core in range(2)], 0))
    offsets = product(forc16[...], ct_h[...], ct_l[...]) + product(obs16[...], gain_h[...], gain_l[...], True)
    off8[...] = offsets[:8]

    row_id = lax.broadcasted_iota(jnp.int32, (N, N), 0)
    col_id = lax.broadcasted_iota(jnp.int32, (N, N), 1)

    def step_first(ks):
        place = first.s[ks]
        raw = jnp.concatenate([ga[core, place, spot] for spot in range(4) for core in range(2)], 0)
        raw = raw + jnp.where(row_id == col_id, ret8[pl.ds(2 * place, 1), :], 0.0)
        put_split(b_h, b_l, 2 * place, product(raw, ct_h[...], ct_l[...]))

    def step_other(ks):
        place = other.s[ks]
        raw = jnp.concatenate(
            [
                gb[core, place, spot]
                + jnp.where(
                    rows_of + (place * 96 + core * W) == cols_of, ret8[pl.ds(2 * spot + 1, 1), :], 0.0
                )
                for spot in range(4)
                for core in range(2)
            ],
            0,
        )
        high, low = split(product(raw, ct_h[...], ct_l[...]))
        target = pl.ds(pl.multiple_of(place * 96, 32), 96)
        for spot in range(4):
            b_h[2 * spot + 1, target, :] = high[96 * spot : 96 * (spot + 1)]
            b_l[2 * spot + 1, target, :] = low[96 * spot : 96 * (spot + 1)]

    def ready(gather, ks):
        for kf in range(4):
            gather.shared(kf, ks)

    ready(first, 0)
    step_first(0)
    first.second_near(1)
    other.second_near(1)
    ready(other, 0)
    step_other(0)
    first.second_near(2)
    other.second_near(2)

    @pl.when(y == 0)
    def _():
        high, low = split(pf_v[...])
        put_split(p_h, p_l, ..., product(pf_v[...], high, low, True))

    first.second_near(3)
    other.second_near(3)
    ready(first, 1)
    step_first(1)
    first.second_far(0)
    other.second_far(0)
    ready(first, 2)
    step_first(2)
    first.second_far(1)
    other.second_far(1)
    ready(other, 1)
    step_other(1)
    first.second_far(2)
    other.second_far(2)
    ready(other, 2)
    step_other(2)
    first.second_far(3)
    other.second_far(3)
    ready(first, 3)
    step_first(3)
    ready(other, 3)
    step_other(3)

    row32 = lax.broadcasted_iota(jnp.int32, (32, N), 0)
    col32 = lax.broadcasted_iota(jnp.int32, (32, N), 1)
    start24 = (z * 4 + x) * CR
    walk = ((row32 < CR) & (row32 + start24 == col32)).astype(F32)
    for j in range(7, -1, -1):
        wc[j] = walk
        walk = product(walk, b_h[j], b_l[j], True)
    left = wc[...].reshape(256, N)
    spread = product(left, ct_h[...], ct_l[...], True).reshape(8, 32, N) * noise8[...].reshape(8, 1, N)
    noise = product(spread.reshape(256, N), ct_h[...], ct_l[...]) + product(left, fix_h[...], fix_l[...])
    gc[...] = noise.reshape(8, 32, N)

    @pl.when(y == 0)
    def _():
        begin = product(walk, p_h[...], p_l[...])
        stage[0] = jnp.where(row32 == CR, pm_v[...], begin)

    @pl.when(y != 0)
    def _():
        stage[0] = jnp.zeros((32, N), F32)

    grown = stage[0]
    for j in range(8):
        grown = product(grown, b_h[j], b_l[j])
        grown = grown + gc[j] + jnp.where(row32 == CR, off8[pl.ds(j, 1), :], 0.0)
    stage[1] = walk
    stage[2] = grown
    kind = 1 + c

    def ship(index, source, target, slot, device):
        return pltpu.make_async_remote_copy(
            src_ref=source,
            dst_ref=target,
            send_sem=send_y.at[index],
            recv_sem=recv_y.at[slot],
            device_id=device,
            device_id_type=MESH,
        )

    mine_a, mine_b = ea.at[c, z, x], eb.at[c, x, z]

    @pl.when(y == 0)
    def _():
        copies = []
        for d in range(3):
            copies.append(ship(3 * d, stage.at[2, pl.ds(8 - 8 * c + 0, 8)], mine_a.at[pl.ds(CR, 8)], 0, y_to[d]))
            copies.append(ship(3 * d + 1, stage.at[2, pl.ds(16, 8)], mine_b.at[pl.ds(CR, 8)], 1, y_to[d]))
            copies.append(ship(3 * d + 2, stage.at[2, pl.ds(CR, 8)], near_mean.at[0], 4, y_to[d]))
        for copy in copies:
            copy.start()
        for copy in copies:
            copy.wait_send()

    @pl.when(y == 1)
    def _():
        copies = []
        for d in range(2):
            copies.append(ship(2 * d, stage.at[kind, pl.ds(0, CR)], mine_a.at[pl.ds(0, CR)], 2, y_to[d]))
            copies.append(ship(2 * d + 1, stage.at[2, pl.ds(CR, 8)], near_mean.at[1], 5, y_to[d]))
        for copy in copies:
            copy.start()
        for copy in copies:
            copy.wait_send()

    @pl.when(y == 2)
    def _():
        copies = [
            ship(0, stage.at[kind, pl.ds(0, CR)], mine_b.at[pl.ds(0, CR)], 3, y_to[0]),
            ship(1, stage.at[2, pl.ds(CR, 8)], near_mean.at[2], 6, y_to[0]),
        ]
        for copy in copies:
            copy.start()
        for copy in copies:
            copy.wait_send()

    @pl.when(y >= 1)
    def _():
        ship(0, mine_a.at[pl.ds(CR, 8)], mine_a.at[pl.ds(CR, 8)], 0, partner).wait_recv()
        ship(0, mine_b.at[pl.ds(CR, 8)], mine_b.at[pl.ds(CR, 8)], 1, partner).wait_recv()
        ship(0, near_mean.at[0], near_mean.at[0], 4, partner).wait_recv()

    @pl.when(y >= 2)
    def _():
        ship(0, mine_a.at[pl.ds(0, CR)], mine_a.at[pl.ds(0, CR)], 2, partner).wait_recv()
        ship(0, near_mean.at[1], near_mean.at[1], 5, partner).wait_recv()

    @pl.when(y >= 3)
    def _():
        ship(0, mine_b.at[pl.ds(0, CR)], mine_b.at[pl.ds(0, CR)], 3, partner).wait_recv()
        ship(0, near_mean.at[2], near_mean.at[2], 6, partner).wait_recv()

    third = PlaneGather(lambda core, f, s: ea.at[core, s, f], 32, c, x, z, x_to, z_to, partner, send3, recv3, 0, sent)
    fourth = PlaneGather(
        lambda core, f, s: eb.at[core, s, f], 32, c, z, x, z_to, x_to, partner, send3, recv3, PER_CLASS, sent
    )
    for gather in (third, fourth):
        gather.first_own(gather.at(0, 0))
    for gather in (third, fourth):
        gather.second(0)
        gather.share(0, 0)

    last = 2 * z + 1
    wf[last, pl.ds(W, W), :] = eye_rows
    behind = product(eye_rows, b_h[last], b_l[last], True)
    w0_s[pl.ds(0, W), :] = eye_rows
    w0_s[pl.ds(W, W), :] = behind

    third.first_near()
    fourth.first_near()

    @pl.loop(0, 2 * z + 1)
    def _(i):
        j = 2 * z - i
        rows = w0_s[...]
        wf[j] = rows
        w0_s[...] = product(rows, b_h[j], b_l[j], True)

    third.second_near(0)
    fourth.second_near(0)
    third.first_far()
    fourth.first_far()

    def noise_rows(part):
        span = pl.ds(4 * part, 4)
        rows = wf[span].reshape(N, N)
        wide = product(rows, ct_h[...], ct_l[...], True).reshape(4, 96, N)
        wide = wide * noise8[pl.ds(4 * part, 4), :].reshape(4, 1, N)
        value = product(wide.reshape(N, N), ct_h[...], ct_l[...]) + product(rows, fix_h[...], fix_l[...])
        gf[span] = value.reshape(4, 96, N)

    noise_rows(0)
    for kf in (1, 2):
        third.second_near(kf)
        fourth.second_near(kf)

    @pl.when(z >= 2)
    def _():
        noise_rows(1)

    third.second_near(3)
    fourth.second_near(3)
    for kf in range(4):
        third.second_far(kf)
        fourth.second_far(kf)
    for ks in range(4):
        ready(third, ks)
        ready(fourth, ks)

    spots = [(a, b) for a in range(4) for b in range(4)]

    @pl.when(y == 3)
    def _():
        put_split(t2_h, t2_l, ..., jnp.concatenate([eb[0, b, a, pl.ds(0, CR), :] for a, b in spots], 0))
        put_split(n2_h, n2_l, ..., jnp.concatenate([eb[1, b, a, pl.ds(0, CR), :] for a, b in spots], 0))
        v2_s[...] = product(w0_s[...], t2_h[...], t2_l[...])

    @pl.when(y != 3)
    def _():
        v2_s[...] = w0_s[...]

    @pl.when(y >= 2)
    def _():
        put_split(t1_h, t1_l, ..., jnp.concatenate([ea[0, a, b, pl.ds(0, CR), :] for a, b in spots], 0))
        put_split(n1_h, n1_l, ..., jnp.concatenate([ea[1, a, b, pl.ds(0, CR), :] for a, b in spots], 0))
        v1_s[...] = product(v2_s[...], t1_h[...], t1_l[...])

    @pl.when(y < 2)
    def _():
        v1_s[...] = v2_s[...]

    @pl.when(y >= 1)
    def _():
        parts = []
        for a, b in spots:
            parts += [ea[1, a, b, pl.ds(CR, 8), :], ea[0, a, b, pl.ds(CR, 8), :], eb[0, b, a, pl.ds(CR, 8), :]]
        put_split(p_h, p_l, ..., jnp.concatenate(parts, 0))

    row16 = lax.broadcasted_iota(jnp.int32, (16, N), 0)

    def mean_rows(row):
        return jnp.where(row16 == 0, row, 0.0)

    xs[pl.ds(0, 96), :] = product(v1_s[...], p_h[...], p_l[...])

    @pl.when(y == 0)
    def _():
        xs[pl.ds(96, 16), :] = mean_rows(pm_v[...])

    @pl.when(y >= 1)
    def _():
        xs[pl.ds(96, 16), :] = mean_rows(near_mean[0, pl.ds(0, 1), :])

    @pl.when(y >= 2)
    def _():
        value = product(xs[...], t1_h[...], t1_l[...], True)
        added = product(v2_s[...], n1_h[...], n1_l[...])
        xs[...] = value + jnp.concatenate([added, mean_rows(near_mean[1, pl.ds(0, 1), :])], 0)

    @pl.when(y >= 3)
    def _():
        value = product(xs[...], t2_h[...], t2_l[...], True)
        added = product(w0_s[...], n2_h[...], n2_l[...])
        xs[...] = value + jnp.concatenate([added, mean_rows(near_mean[2, pl.ds(0, 1), :])], 0)

    @pl.loop(0, 2 * z + 1)
    def _(j):
        value = product(xs[...], b_h[j], b_l[j])
        xs[...] = value + jnp.concatenate([gf[j], mean_rows(off8[pl.ds(j, 1), :])], 0)

    covariances[0] = xs[pl.ds(0, W), :]
    means[pl.ds(0, 1), :] = xs[pl.ds(96, 1), :]
    value = product(xs[pl.ds(W, 64), :], b_h[last], b_l[last])
    covariances[1] = value[:W] + gf[last, pl.ds(W, W), :]
    means[pl.ds(1, 1), :] = value[W : W + 1] + off8[pl.ds(last, 1), :]

    for copy in sent:
        copy.wait_send()


def vmem(shape, dtype=F32):
    return pltpu.VMEM(shape, dtype)


def pair(shape):
    return [vmem(shape, BF16), vmem(shape, BF16)]


def per_device(mixing, retention, forcing, observations, model_noise, obs_noise, gain, obs_t, prior_mean, prior_factor):
    dma = pltpu.SemaphoreType.DMA
    square = (N, N)
    return pl.pallas_call(
        kernel,
        out_shape=(jax.ShapeDtypeStruct((2, N), F32), jax.ShapeDtypeStruct((2, W, N), F32)),
        in_specs=[pl.BlockSpec(memory_space=pl.ANY)] * 10,
        out_specs=(pl.BlockSpec(memory_space=pltpu.VMEM),) * 2,
        scratch_shapes=[
            vmem((2, 4, 4, W, N)),
            vmem((2, 4, 4, W, N)),
            vmem((2, 4, W, N)),
            vmem((2, 4, 4, 32, N)),
            vmem((2, 4, 4, 32, N)),
            vmem((4, 2, N)),
            vmem((4, 2, N)),
            vmem((4, 2, NOBS)),
            vmem((4, 2, N)),
            vmem((8, N)),
            vmem((16, N)),
            vmem((16, NOBS)),
            vmem((8, N)),
            vmem((1, NOBS)),
            vmem((N, NOBS)),
            *pair((N, NOBS)),
            vmem((W, NOBS)),
            vmem((1, N)),
            vmem(square),
            *pair(square),
            *pair(square),
            *pair(square),
            *pair((8, N, N)),
            vmem((8, N)),
            vmem((8, 32, N)),
            vmem((8, 32, N)),
            vmem((8, 96, N)),
            vmem((8, 96, N)),
            vmem((3, 32, N)),
            vmem((8, N)),
            vmem((3, 8, N)),
            *pair(square),
            *pair(square),
            *pair(square),
            *pair(square),
            vmem((96, N)),
            vmem((96, N)),
            vmem((96, N)),
            vmem((112, N)),
            dma((2 * PER_CLASS,)),
            dma((2 * PER_CLASS,)),
            dma((2 * PER_CLASS,)),
            dma((2 * PER_CLASS,)),
            dma((7,)),
            dma((7,)),
            dma((12,)),
            dma((12,)),
            dma((9,)),
            dma((7,)),
            dma((11,)),
        ],
        compiler_params=pltpu.CompilerParams(
            collective_id=0, has_side_effects=True, vmem_limit_bytes=67043328
        ),
        name="prefix",
    )(
        mixing, retention, forcing, observations, model_noise, obs_noise.reshape(1, NOBS), gain, obs_t,
        prior_mean.reshape(1, N), prior_factor,
    )


def solution(mesh):
    grid = Mesh(mesh.devices.reshape(4, 4, 4, 2), SEG + COL)
    placed = (
        P(SEG, COL, None),
        P(SEG, None),
        P(SEG, None),
        P(SEG, None),
        P(SEG, None),
        P(),
        P(),
        P(COL, None),
        P(),
        P(),
    )
    return jax.shard_map(
        per_device,
        mesh=grid,
        in_specs=placed,
        out_specs=(P(SEG, None), P(SEG, COL, None)),
        check_vma=False,
    )
```

profile of v0, /device:TPU:25, one launch (start us, length us, event | category | flops | bytes accessed | tf_op | source)
XLA Modules:
  0.0 65.7 jit_solution(14163101320982618990)
XLA Ops:
  0.6 1.2 %reshape.11.prior_mean = f32[1,384]{1,0:T(1,128)} reshape(f32[384]{0:T(512)} %param.18) | data formatting | bytes 3072 | tf_op jit(solution)/shard_map/reshape | solution.py:651
  1.9 61.0 %prefix.1 = (f32[2,384]{1,0:T(2,128)}, f32[2,48,384]{2,1,0:T(8,128)}) custom-call(f32[2,48,384]{2,1,0:T(8,128)} %mixing.1, f32[2,384]{1,0:T(2,128)} %retention.1, f32[2,384]{1,0:T(2,128)} %forcing.1, f32[2,1024]{1,0:T(2,128)} %observations.1, f32[2,384]{1,0:T(2,128)} %model_noise.1, f32[1,1024]{1,0:T(1,128)} %bitcast.1, f32[384,1024]{1,0:T(8,128)} %gain.1, ...), custom_call_target="tpu_custom_call" | custom-call | tf_op jit(solution)/shard_map/prefix/pallas_call | solution.py:588
  62.9 1.2 %copy.14 = f32[2,384]{1,0:T(2,128)} copy(f32[2,384]{1,0:T(2,128)} %get-tuple-element.4) | data formatting | bytes 6144
  64.1 1.6 %copy.15 = f32[2,48,384]{2,1,0:T(8,128)} copy(f32[2,48,384]{2,1,0:T(8,128)} %get-tuple-element.5) | data formatting | bytes 294912
where the time goes:
time: 65.9 us; the launch traced here: 65.7 us
  Pallas kernels  61 us (93%)
  local copies, waits for them, and re-layouts  4.06 us (6%)
    pallas_call x1, Pallas kernels, per_device(): pl.pallas_call(kernel, out_shape=(jax.ShapeDtypeStruct((2, N), F32), jax....  61 us
    unnamed x2, local copies, waits for them, and re-layouts  2.81 us

commit v1 on v0

v1 whole, which is shorter than its diff:
```python
import functools

import jax
import jax.numpy as jnp
from jax import lax
from jax.experimental import pallas as pl
from jax.experimental.pallas import tpu as pltpu
from jax.sharding import Mesh
from jax.sharding import PartitionSpec as P

MESH = pl.DeviceIdType.MESH
F32 = jnp.float32
BF16 = jnp.bfloat16
SEG = ("y", "z")
COL = ("x", "c")
N = 384
NOBS = 1024
W = 48
CR = 24
PER_CLASS = 36
STRAIGHT1 = (3,)
STRAIGHT3 = (0, 1, 2, 3)


def split(value):
    high = value.astype(BF16)
    low = (value - high.astype(F32)).astype(BF16)
    return high, low


def dot(left, right, transposed):
    dims = (((1,), (1 if transposed else 0,)), ((), ()))
    return lax.dot_general(left, right, dims, preferred_element_type=F32)


def product(left, right_high, right_low, transposed=False):
    high, low = split(left)
    rows = left.shape[0]
    both = dot(jnp.concatenate([high, low], 0), right_high, transposed)
    return both[:rows] + (both[rows:] + dot(high, right_low, transposed))


def put_split(high_ref, low_ref, index, value):
    high, low = split(value)
    high_ref[index] = high
    low_ref[index] = low


def turn(position, by):
    return lax.rem(position + (by % 4), 4)


class PlaneGather:
    def __init__(self, unit, rows, core, first, second, to_first, to_second, partner, send, recv, base, sent, straight):
        self.unit, self.rows, self.core = unit, rows, core
        self.f = [turn(first, d) for d in (0, -1, 1, 2)]
        self.s = [turn(second, d) for d in (0, -1, 1, 2)]
        self.to_first, self.to_second, self.partner = to_first, to_second, partner
        self.send, self.recv, self.base, self.sent, self.straight = send, recv, base, sent, straight

    def at(self, kf, ks, half=None, core=None):
        ref = self.unit(self.core if core is None else core, self.f[kf], self.s[ks])
        if half is None:
            return ref
        middle = self.rows // 16 * 8
        return ref.at[pl.ds(0, middle)] if half == 0 else ref.at[pl.ds(middle, self.rows - middle)]

    def start(self, index, source, target, device):
        copy = pltpu.make_async_remote_copy(
            src_ref=source,
            dst_ref=target,
            send_sem=self.send.at[self.base + index],
            recv_sem=self.recv.at[self.base + index],
            device_id=device,
            device_id_type=MESH,
        )
        copy.start()
        self.sent.append(copy)

    def arrive(self, index, slot):
        pltpu.make_async_remote_copy(
            src_ref=slot,
            dst_ref=slot,
            send_sem=self.send.at[self.base + index],
            recv_sem=self.recv.at[self.base + index],
            device_id=self.partner,
            device_id_type=MESH,
        ).wait_recv()

    def first_own(self, source):
        for way in (0, 1):
            self.start(way, source, self.at(0, 0), self.to_first[way])

    def first_own_far(self, source):
        self.start(2, source, self.at(0, 0), self.to_first[2])

    def share(self, kf, ks, source=None):
        slot = self.at(kf, ks)
        self.start(20 + 4 * ks + kf, slot if source is None else source, slot, self.partner)

    def shared(self, kf, ks):
        self.arrive(20 + 4 * ks + kf, self.at(kf, ks, core=1 - self.core))

    def second(self, kf, source=None):
        slot = self.at(kf, 0)
        source = slot if source is None else source
        for way in (0, 1):
            self.start(4 + 2 * kf + way, source, slot, self.to_second[way])
        if kf in self.straight:
            self.start(12 + 2 * kf, source, slot, self.to_second[2])

    def first_near(self):
        for way in (0, 1):
            self.arrive(way, self.at(1 + way, 0))
            self.second(1 + way)
            self.share(1 + way, 0)

    def first_far(self):
        self.arrive(2, self.at(3, 0))
        self.second(3)
        self.share(3, 0)

    def second_near(self, kf):
        for way in (0, 1):
            self.arrive(4 + 2 * kf + way, self.at(kf, 1 + way))
            if kf not in self.straight:
                part = self.at(kf, 1 + way, half=way)
                self.start(12 + 2 * kf + way, part, part, self.to_second[way])
            self.share(kf, 1 + way)

    def second_far(self, kf):
        if kf in self.straight:
            self.arrive(12 + 2 * kf, self.at(kf, 3))
        else:
            for way in (0, 1):
                self.arrive(12 + 2 * kf + way, self.at(kf, 3, half=way))
        self.share(kf, 3)


def kernel(
    mixing, retention, forcing, observations, model_noise, obs_noise, gain, obs_t, prior_mean, prior_factor,
    out,
    ga, gb, cg, ea, eb, ret4, forc4, obs4, noise4, ret8, forc16, obs16, noise8, on_v, gain_v, gain_h, gain_l,
    obs_v, pm_v, pf_v, ct_h, ct_l, fix_h, fix_l, p_h, p_l, b_h, b_l, off8, wc, gc, wf, gf, stage,
    near_mean, t1_h, t1_l, n1_h, n1_l, t2_h, t2_l, n2_h, n2_l, w0_s, v1_s, v2_s, xs,
    send1, recv1, send3, recv3, send_c, recv_c, send_g, recv_g, send_s, recv_s, send_y, recv_y, send_m, recv_m, local,
):
    y, z, x, c = (lax.axis_index(name) for name in ("y", "z", "x", "c"))
    partner = (y, z, x, 1 - c)
    x_to = [(y, z, turn(x, d), c) for d in (1, -1, 2)]
    z_to = [(y, turn(z, d), x, c) for d in (1, -1, 2)]
    y_to = [(turn(y, d), z, x, c) for d in (1, 2, 3)]
    sent = []

    own = {}
    for index, (name, source, target) in enumerate(
        (
            ("gain", gain, gain_v),
            ("obs_t", obs_t, obs_v),
            ("mix0", mixing.at[0], ga.at[c, z, x]),
            ("mix1", mixing.at[1], gb.at[c, x, z]),
            ("noise", obs_noise, on_v),
            ("ret", retention, ret4.at[z]),
            ("forc", forcing, forc4.at[z]),
            ("obs", observations, obs4.at[z]),
            ("mn", model_noise, noise4.at[z]),
            ("pm", prior_mean, pm_v),
            ("pf", prior_factor, pf_v),
        )
    ):
        own[name] = pltpu.make_async_copy(source, target, local.at[index])
        own[name].start()

    ea[c, z, x] = jnp.zeros((CR, N), F32)
    eb[c, x, z] = jnp.zeros((CR, N), F32)
    forc16[...] = jnp.zeros((16, N), F32)
    obs16[...] = jnp.zeros((16, NOBS), F32)

    barrier = pltpu.get_barrier_semaphore()
    friends = [partner] + x_to + z_to + y_to
    for friend in friends:
        pl.semaphore_signal(barrier, inc=1, device_id=friend, device_id_type=MESH)

    own["gain"].wait()
    own["obs_t"].wait()
    own["noise"].wait()
    put_split(gain_h, gain_l, ..., gain_v[...])
    rows_of = lax.broadcasted_iota(jnp.int32, (W, N), 0)
    cols_of = lax.broadcasted_iota(jnp.int32, (W, N), 1)
    start_row = x * 96 + c * W
    eye_rows = (rows_of + start_row == cols_of).astype(F32)
    cg[c, x] = eye_rows - product(obs_v[...], gain_h[...], gain_l[...], True)
    for part in range(3):
        rows = pl.ds(part * 128, 128)
        put_split(fix_h, fix_l, rows, product(gain_v[rows, :] * on_v[...], gain_h[...], gain_l[...], True))

    own["pf"].wait()

    @pl.when(y == 0)
    def _():
        high, low = split(pf_v[...])
        put_split(p_h, p_l, ..., product(pf_v[...], high, low, True))

    pl.semaphore_wait(barrier, len(friends))

    first = PlaneGather(lambda core, f, s: ga.at[core, s, f], W, c, x, z, x_to, z_to, partner, send1, recv1, 0, sent, STRAIGHT1)
    other = PlaneGather(
        lambda core, f, s: gb.at[core, s, f], W, c, z, x, z_to, x_to, partner, send1, recv1, PER_CLASS, sent, STRAIGHT1
    )

    def gain_copy(index, slot, device):
        return pltpu.make_async_remote_copy(
            src_ref=slot,
            dst_ref=slot,
            send_sem=send_c.at[index],
            recv_sem=recv_c.at[index],
            device_id=device,
            device_id_type=MESH,
        )

    def third_of(place, part):
        return cg.at[c, place, pl.ds(16 * part, 16)]

    @pl.when(y < 3)
    def _():
        for index, device in enumerate(x_to):
            gain_copy(index, third_of(x, y), device).start()

    for gather, step in ((first, 0), (other, 1)):
        gather.first_own(mixing.at[step])
    for gather, step in ((first, 0), (other, 1)):
        gather.first_own_far(mixing.at[step])
    for gather, step in ((first, 0), (other, 1)):
        gather.second(0, mixing.at[step])
    gain_copy(3, cg.at[c, x], partner).start()
    for gather, step in ((first, 0), (other, 1)):
        gather.share(0, 0, mixing.at[step])

    small = []
    for array, (source, target) in enumerate(
        ((retention, ret4), (forcing, forc4), (observations, obs4), (model_noise, noise4))
    ):
        for d in (1, 2, 3):
            index = 3 * array + d - 1
            copy = pltpu.make_async_remote_copy(
                src_ref=source,
                dst_ref=target.at[z],
                send_sem=send_s.at[index],
                recv_sem=recv_s.at[index],
                device_id=(y, turn(z, d), x, c),
                device_id_type=MESH,
            )
            copy.start()
            sent.append(copy)
            slot = target.at[turn(z, -d)]
            small.append(
                pltpu.make_async_remote_copy(
                    src_ref=slot,
                    dst_ref=slot,
                    send_sem=send_s.at[index],
                    recv_sem=recv_s.at[index],
                    device_id=partner,
                    device_id_type=MESH,
                )
            )


    @pl.when(y < 3)
    def _():
        for index, d in enumerate((-1, 1, 2)):
            slot = third_of(turn(x, d), y)
            gain_copy(index, slot, partner).wait_recv()
            for way in range(3):
                copy = pltpu.make_async_remote_copy(
                    src_ref=slot,
                    dst_ref=slot,
                    send_sem=send_g.at[3 * way + index],
                    recv_sem=recv_g.at[3 * y + index],
                    device_id=y_to[way],
                    device_id_type=MESH,
                )
                copy.start()

    def drain():
        for copy in sent:
            copy.wait_send()

        @pl.when(c == 0)
        def _():
            ships(True, lambda copy: copy.wait_send())

        @pl.when(c == 1)
        def _():
            ships(False, lambda copy: copy.wait_send())
            for plane in range(3):

                @pl.when(y > plane)
                def _():
                    pass_mean(plane).wait_send()

        @pl.when(y < 3)
        def _():
            for index, device in enumerate(x_to):
                gain_copy(index, third_of(x, y), device).wait_send()
            for index, d in enumerate((-1, 1, 2)):
                slot = third_of(turn(x, d), y)
                for way in range(3):
                    pltpu.make_async_remote_copy(
                        src_ref=slot,
                        dst_ref=slot,
                        send_sem=send_g.at[3 * way + index],
                        recv_sem=recv_g.at[3 * y + index],
                        device_id=y_to[way],
                        device_id_type=MESH,
                    ).wait_send()

        for index in range(3):
            gain_copy(4 + index, cg.at[c, x], partner).wait_send()
        gain_copy(3, cg.at[c, x], partner).wait_send()

    first.first_near()
    other.first_near()
    first.first_far()
    other.first_far()
    first.second_near(0)
    other.second_near(0)
    for part in range(3):

        @pl.when(y != part)
        def _():
            for index, d in enumerate((-1, 1, 2)):
                slot = third_of(turn(x, d), part)
                pltpu.make_async_remote_copy(
                    src_ref=slot,
                    dst_ref=slot,
                    send_sem=send_g.at[0],
                    recv_sem=recv_g.at[3 * part + index],
                    device_id=partner,
                    device_id_type=MESH,
                ).wait_recv()

    for index, d in enumerate((-1, 1, 2)):
        gain_copy(4 + index, cg.at[c, turn(x, d)], partner).start()

    for name in ("ret", "forc", "obs", "mn", "pm", "mix0", "mix1"):
        own[name].wait()
    for copy in small:
        copy.wait_recv()
    for place in range(4):
        for step in range(2):
            row = 2 * place + step
            ret8[pl.ds(row, 1), :] = ret4[place, pl.ds(step, 1), :]
            noise8[pl.ds(row, 1), :] = noise4[place, pl.ds(step, 1), :]
            forc16[pl.ds(row, 1), :] = forc4[place, pl.ds(step, 1), :]
            obs16[pl.ds(row, 1), :] = obs4[place, pl.ds(step, 1), :]

    gain_copy(3, cg.at[1 - c, x], partner).wait_recv()
    for index, d in enumerate((-1, 1, 2)):
        gain_copy(4 + index, cg.at[1 - c, turn(x, d)], partner).wait_recv()
    put_split(ct_h, ct_l, ..., jnp.concatenate([cg[core, place] for place in range(4) for core in range(2)], 0))
    offsets = product(forc16[...], ct_h[...], ct_l[...]) + product(obs16[...], gain_h[...], gain_l[...], True)
    off8[...] = offsets[:8]

    row_id = lax.broadcasted_iota(jnp.int32, (N, N), 0)
    col_id = lax.broadcasted_iota(jnp.int32, (N, N), 1)

    def step_first(ks):
        place = first.s[ks]
        raw = jnp.concatenate([ga[core, place, spot] for spot in range(4) for core in range(2)], 0)
        raw = raw + jnp.where(row_id == col_id, ret8[pl.ds(2 * place, 1), :], 0.0)
        put_split(b_h, b_l, 2 * place, product(raw, ct_h[...], ct_l[...]))

    def step_other(ks):
        place = other.s[ks]
        raw = jnp.concatenate(
            [
                gb[core, place, spot]
                + jnp.where(
                    rows_of + (place * 96 + core * W) == cols_of, ret8[pl.ds(2 * spot + 1, 1), :], 0.0
                )
                for spot in range(4)
                for core in range(2)
            ],
            0,
        )
        high, low = split(product(raw, ct_h[...], ct_l[...]))
        target = pl.ds(pl.multiple_of(place * 96, 32), 96)
        for spot in range(4):
            b_h[2 * spot + 1, target, :] = high[96 * spot : 96 * (spot + 1)]
            b_l[2 * spot + 1, target, :] = low[96 * spot : 96 * (spot + 1)]

    def ready(gather, ks):
        for kf in range(4):
            gather.shared(kf, ks)

    ready(first, 0)
    step_first(0)
    first.second_near(1)
    other.second_near(1)
    ready(other, 0)
    step_other(0)
    first.second_near(2)
    other.second_near(2)

    first.second_near(3)
    other.second_near(3)
    ready(first, 1)
    step_first(1)
    first.second_far(0)
    other.second_far(0)
    ready(first, 2)
    step_first(2)
    first.second_far(1)
    other.second_far(1)
    ready(other, 1)
    step_other(1)
    first.second_far(2)
    other.second_far(2)
    ready(other, 2)
    step_other(2)
    first.second_far(3)
    other.second_far(3)
    ready(first, 3)
    step_first(3)
    ready(other, 3)
    step_other(3)

    row32 = lax.broadcasted_iota(jnp.int32, (32, N), 0)
    col32 = lax.broadcasted_iota(jnp.int32, (32, N), 1)
    start24 = (z * 4 + x) * CR
    walk = ((row32 < CR) & (row32 + start24 == col32)).astype(F32)
    for j in range(7, -1, -1):
        wc[j] = walk
        walk = product(walk, b_h[j], b_l[j], True)
    stage[1] = walk
    mine_a, mine_b = ea.at[c, z, x], eb.at[c, x, z]

    def ship(index, source, target, slot, device):
        return pltpu.make_async_remote_copy(
            src_ref=source,
            dst_ref=target,
            send_sem=send_y.at[index],
            recv_sem=recv_y.at[slot],
            device_id=device,
            device_id_type=MESH,
        )

    def ships(first_core, act):
        near, far = pl.ds(0, 256), pl.ds(256, 128)
        if first_core:

            @pl.when(y == 1)
            def _():
                for d in range(2):
                    act(ship(d, stage.at[1, pl.ds(0, CR)], mine_a, 2, y_to[d]))

            @pl.when(y == 2)
            def _():
                act(ship(0, stage.at[1, pl.ds(0, CR)], mine_b, 3, y_to[0]))

            return
        packed, mean = stage.at[2, pl.ds(0, CR)], stage.at[0, pl.ds(CR, 8)]

        @pl.when(y == 0)
        def _():
            for d in range(3):
                act(ship(3 * d, packed.at[:, pl.ds(0, 128)], mine_a.at[:, far], 0, y_to[d]))
                act(ship(3 * d + 1, packed.at[:, pl.ds(128, 128)], mine_b.at[:, far], 1, y_to[d]))
                act(ship(3 * d + 2, mean, near_mean.at[0], 4, y_to[d]))

        @pl.when(y == 1)
        def _():
            for d in range(2):
                act(ship(2 * d, packed.at[:, near], mine_a.at[:, near], 2, y_to[d]))
                act(ship(2 * d + 1, mean, near_mean.at[1], 5, y_to[d]))

        @pl.when(y == 2)
        def _():
            act(ship(0, packed.at[:, near], mine_b.at[:, near], 3, y_to[0]))
            act(ship(1, mean, near_mean.at[2], 6, y_to[0]))

    def pass_mean(index):
        return pltpu.make_async_remote_copy(
            src_ref=near_mean.at[index],
            dst_ref=near_mean.at[index],
            send_sem=send_m.at[index],
            recv_sem=recv_m.at[index],
            device_id=partner,
            device_id_type=MESH,
        )

    @pl.when(c == 0)
    def _():
        ships(True, lambda copy: copy.start())

    @pl.when(c == 1)
    def _():
        left = wc[...].reshape(256, N)
        spread = product(left, ct_h[...], ct_l[...], True).reshape(8, 32, N) * noise8[...].reshape(8, 1, N)
        noise = product(spread.reshape(256, N), ct_h[...], ct_l[...]) + product(left, fix_h[...], fix_l[...])
        gc[...] = noise.reshape(8, 32, N)

        @pl.when(y == 0)
        def _():
            begin = product(stage[1], p_h[...], p_l[...])
            stage[0] = jnp.where(row32 == CR, pm_v[...].reshape(1, N), begin)

        @pl.when(y != 0)
        def _():
            stage[0] = jnp.zeros((32, N), F32)

        grown = stage[0]
        for j in range(8):
            grown = product(grown, b_h[j], b_l[j])
            grown = grown + gc[j] + jnp.where(row32 == CR, off8[pl.ds(j, 1), :], 0.0)
        stage[0] = grown
        band = row32[:, :128] + start24
        low, high = band < 128, band >= 256
        one, two, three = (grown[:, 128 * b : 128 * (b + 1)] for b in range(3))
        stage[2, :, pl.ds(0, 128)] = jnp.where(low, one, jnp.where(high, three, two))
        stage[2, :, pl.ds(128, 128)] = jnp.where(low, two, jnp.where(high, one, three))
        ships(False, lambda copy: copy.start())

    @pl.when((c == 0) & (y >= 2))
    def _():
        ship(0, mine_a, mine_a, 2, partner).wait_recv()

    @pl.when((c == 0) & (y >= 3))
    def _():
        ship(0, mine_b, mine_b, 3, partner).wait_recv()

    @pl.when((c == 1) & (y >= 1))
    def _():
        ship(0, mine_a.at[:, pl.ds(256, 128)], mine_a.at[:, pl.ds(256, 128)], 0, partner).wait_recv()
        ship(0, mine_b.at[:, pl.ds(256, 128)], mine_b.at[:, pl.ds(256, 128)], 1, partner).wait_recv()

    @pl.when((c == 1) & (y >= 2))
    def _():
        ship(0, mine_a.at[:, pl.ds(0, 256)], mine_a.at[:, pl.ds(0, 256)], 2, partner).wait_recv()

    @pl.when((c == 1) & (y >= 3))
    def _():
        ship(0, mine_b.at[:, pl.ds(0, 256)], mine_b.at[:, pl.ds(0, 256)], 3, partner).wait_recv()

    third = PlaneGather(lambda core, f, s: ea.at[core, s, f], CR, c, x, z, x_to, z_to, partner, send3, recv3, 0, sent, STRAIGHT3)
    fourth = PlaneGather(
        lambda core, f, s: eb.at[core, s, f], CR, c, z, x, z_to, x_to, partner, send3, recv3, PER_CLASS, sent, STRAIGHT3
    )
    for gather in (third, fourth):
        gather.first_own(gather.at(0, 0))
    for gather in (third, fourth):
        gather.first_own_far(gather.at(0, 0))
    for gather in (third, fourth):
        gather.second(0)
        gather.share(0, 0)

    for plane in range(3):

        @pl.when((c == 1) & (y > plane))
        def _():
            ship(0, near_mean.at[plane], near_mean.at[plane], 4 + plane, partner).wait_recv()
            pass_mean(plane).start()

    last = 2 * z + 1
    wf[last, pl.ds(W, W), :] = eye_rows
    behind = product(eye_rows, b_h[last], b_l[last], True)
    w0_s[pl.ds(0, W), :] = eye_rows
    w0_s[pl.ds(W, W), :] = behind

    third.first_near()
    fourth.first_near()
    third.first_far()
    fourth.first_far()

    @pl.loop(0, 2 * z + 1)
    def _(i):
        j = 2 * z - i
        rows = w0_s[...]
        wf[j] = rows
        w0_s[...] = product(rows, b_h[j], b_l[j], True)

    def noise_rows(part):
        span = pl.ds(4 * part, 4)
        rows = wf[span].reshape(N, N)
        wide = product(rows, ct_h[...], ct_l[...], True).reshape(4, 96, N)
        wide = wide * noise8[pl.ds(4 * part, 4), :].reshape(4, 1, N)
        value = product(wide.reshape(N, N), ct_h[...], ct_l[...]) + product(rows, fix_h[...], fix_l[...])
        gf[span] = value.reshape(4, 96, N)

    third.second_near(0)
    fourth.second_near(0)
    noise_rows(0)
    for kf in (1, 2):
        third.second_near(kf)
        fourth.second_near(kf)

    @pl.when(z >= 2)
    def _():
        noise_rows(1)

    third.second_near(3)
    fourth.second_near(3)
    for kf in range(4):
        third.second_far(kf)
        fourth.second_far(kf)
    for ks in range(4):
        ready(third, ks)
        ready(fourth, ks)

    spots = [(a, b) for a in range(4) for b in range(4)]

    for plane in range(3):

        @pl.when((c == 0) & (y > plane))
        def _():
            pass_mean(plane).wait_recv()

    def symmetric(own, after):
        d0, d1, d2 = (own[128 * b : 128 * (b + 1)] for b in range(3))
        u0, u1, u2 = (after[128 * b : 128 * (b + 1)] for b in range(3))
        rows = ((d0, u0, u2.T), (u0.T, d1, u1), (u2, u1.T, d2))
        return jnp.concatenate([jnp.concatenate(row, 1) for row in rows], 0)

    def columns(pick, block):
        return jnp.concatenate([pick(a, b)[:, 128 * block : 128 * (block + 1)] for a, b in spots], 0)

    def from_a(a, b):
        return ea[1, a, b]

    def from_b(a, b):
        return eb[1, b, a]

    @pl.when(y == 3)
    def _():
        put_split(t2_h, t2_l, ..., jnp.concatenate([eb[0, b, a] for a, b in spots], 0))
        put_split(n2_h, n2_l, ..., symmetric(columns(from_b, 0), columns(from_b, 1)))
        v2_s[...] = product(w0_s[...], t2_h[...], t2_l[...])

    @pl.when(y != 3)
    def _():
        v2_s[...] = w0_s[...]

    @pl.when(y >= 2)
    def _():
        put_split(t1_h, t1_l, ..., jnp.concatenate([ea[0, a, b] for a, b in spots], 0))
        put_split(n1_h, n1_l, ..., symmetric(columns(from_a, 0), columns(from_a, 1)))
        v1_s[...] = product(v2_s[...], t1_h[...], t1_l[...])

    @pl.when(y < 2)
    def _():
        v1_s[...] = v2_s[...]

    @pl.when(y >= 1)
    def _():
        put_split(p_h, p_l, ..., symmetric(columns(from_a, 2), columns(from_b, 2)))

    row16 = lax.broadcasted_iota(jnp.int32, (16, N), 0)

    def mean_rows(row):
        return jnp.where(row16 == 0, row, 0.0)

    xs[pl.ds(0, 96), :] = product(v1_s[...], p_h[...], p_l[...])

    @pl.when(y == 0)
    def _():
        xs[pl.ds(96, 16), :] = mean_rows(pm_v[...].reshape(1, N))

    @pl.when(y >= 1)
    def _():
        xs[pl.ds(96, 16), :] = mean_rows(near_mean[0, pl.ds(0, 1), :])

    @pl.when(y >= 2)
    def _():
        value = product(xs[...], t1_h[...], t1_l[...], True)
        added = product(v2_s[...], n1_h[...], n1_l[...])
        xs[...] = value + jnp.concatenate([added, mean_rows(near_mean[1, pl.ds(0, 1), :])], 0)

    @pl.when(y >= 3)
    def _():
        value = product(xs[...], t2_h[...], t2_l[...], True)
        added = product(w0_s[...], n2_h[...], n2_l[...])
        xs[...] = value + jnp.concatenate([added, mean_rows(near_mean[2, pl.ds(0, 1), :])], 0)

    @pl.loop(0, 2 * z + 1)
    def _(j):
        value = product(xs[...], b_h[j], b_l[j])
        xs[...] = value + jnp.concatenate([gf[j], mean_rows(off8[pl.ds(j, 1), :])], 0)

    out[pl.ds(0, W), :] = xs[pl.ds(0, W), :]
    out[pl.ds(96, 1), :] = xs[pl.ds(96, 1), :]
    value = product(xs[pl.ds(W, 64), :], b_h[last], b_l[last])
    out[pl.ds(W, W), :] = value[:W] + gf[last, pl.ds(W, W), :]
    out[pl.ds(97, 1), :] = value[W : W + 1] + off8[pl.ds(last, 1), :]
    drain()


def finish(rows, means, covariances):
    covariances[0] = rows[pl.ds(0, W), :]
    covariances[1] = rows[pl.ds(W, W), :]
    means[...] = rows[pl.ds(96, 2), :]


def vmem(shape, dtype=F32):
    return pltpu.VMEM(shape, dtype)


def pair(shape):
    return [vmem(shape, BF16), vmem(shape, BF16)]


def per_device(mixing, retention, forcing, observations, model_noise, obs_noise, gain, obs_t, prior_mean, prior_factor):
    dma = pltpu.SemaphoreType.DMA
    square = (N, N)
    rows = pl.pallas_call(
        kernel,
        out_shape=jax.ShapeDtypeStruct((104, N), F32),
        in_specs=[pl.BlockSpec(memory_space=pl.ANY)] * 10,
        out_specs=pl.BlockSpec(memory_space=pltpu.VMEM),
        scratch_shapes=[
            vmem((2, 4, 4, W, N)),
            vmem((2, 4, 4, W, N)),
            vmem((2, 4, W, N)),
            vmem((2, 4, 4, CR, N)),
            vmem((2, 4, 4, CR, N)),
            vmem((4, 2, N)),
            vmem((4, 2, N)),
            vmem((4, 2, NOBS)),
            vmem((4, 2, N)),
            vmem((8, N)),
            vmem((16, N)),
            vmem((16, NOBS)),
            vmem((8, N)),
            vmem((1, NOBS)),
            vmem((N, NOBS)),
            *pair((N, NOBS)),
            vmem((W, NOBS)),
            vmem((N,)),
            vmem(square),
            *pair(square),
            *pair(square),
            *pair(square),
            *pair((8, N, N)),
            vmem((8, N)),
            vmem((8, 32, N)),
            vmem((8, 32, N)),
            vmem((8, 96, N)),
            vmem((8, 96, N)),
            vmem((3, 32, N)),
            vmem((3, 8, N)),
            *pair(square),
            *pair(square),
            *pair(square),
            *pair(square),
            vmem((96, N)),
            vmem((96, N)),
            vmem((96, N)),
            vmem((112, N)),
            dma((2 * PER_CLASS,)),
            dma((2 * PER_CLASS,)),
            dma((2 * PER_CLASS,)),
            dma((2 * PER_CLASS,)),
            dma((7,)),
            dma((7,)),
            dma((9,)),
            dma((9,)),
            dma((12,)),
            dma((12,)),
            dma((9,)),
            dma((7,)),
            dma((3,)),
            dma((3,)),
            dma((11,)),
        ],
        compiler_params=pltpu.CompilerParams(
            collective_id=0, has_side_effects=True, vmem_limit_bytes=67043328
        ),
        name="prefix",
    )(
        mixing, retention, forcing, observations, model_noise, obs_noise.reshape(1, NOBS), gain, obs_t,
        prior_mean, prior_factor,
    )
    return pl.pallas_call(
        finish,
        out_shape=(jax.ShapeDtypeStruct((2, N), F32), jax.ShapeDtypeStruct((2, W, N), F32)),
        in_specs=[pl.BlockSpec(memory_space=pltpu.VMEM)],
        out_specs=(pl.BlockSpec(memory_space=pltpu.VMEM),) * 2,
        name="finish",
    )(rows)


def solution(mesh):
    grid = Mesh(mesh.devices.reshape(4, 4, 4, 2), SEG + COL)
    placed = (
        P(SEG, COL, None),
        P(SEG, None),
        P(SEG, None),
        P(SEG, None),
        P(SEG, None),
        P(),
        P(),
        P(COL, None),
        P(),
        P(),
    )
    return jax.shard_map(
        per_device,
        mesh=grid,
        in_specs=placed,
        out_specs=(P(SEG, None), P(SEG, COL, None)),
        check_vma=False,
    )
```

time: 65.9 us -> 57 us (0.86)
  the two profiles are of different devices: /device:TPU:25 before, /device:TPU:120 now
where the time goes in v1:
time: 57 us; the launch traced here: 56.9 us
  Pallas kernels  56.2 us (99%)
  between operations  0.64 us (1%)
    pallas_call x1, Pallas kernels, per_device(): pl.pallas_call(kernel, out_shape=jax.ShapeDtypeStruct((104, N), F32), in_...  54.7 us
    pallas_call x1, Pallas kernels, per_device(): pl.pallas_call(finish, out_shape=(jax.ShapeDtypeStruct((2, N), F32), jax....  1.59 us

profile of v1, /device:TPU:120, one launch (start us, length us, event | category | flops | bytes accessed | tf_op | source)
XLA Modules:
  0.0 56.9 jit_solution(12056024077199917093)
XLA Ops:
  0.6 54.7 %prefix.1.rows = f32[104,384]{1,0:T(8,128)} custom-call(f32[2,48,384]{2,1,0:T(8,128)} %mixing.1, f32[2,384]{1,0:T(2,128)} %retention.1, f32[2,384]{1,0:T(2,128)} %forcing.1, f32[2,1024]{1,0:T(2,128)} %observations.1, f32[2,384]{1,0:T(2,128)} %model_noise.1, f32[1,1024]{1,0:T(1,128)} %bitcast.1, f32[384,1024]{1,0:T(8,128)} %gain.1, f32[48,1024]{1,0:T(8,128)} %obs_t.1, ...), custom_call_target="tpu_custom_call" | custom-call | tf_op jit(solution)/shard_map/prefix/pallas_call | solution.py:714
  55.3 1.6 %finish.1 = (f32[2,384]{1,0:T(2,128)}, f32[2,48,384]{2,1,0:T(8,128)}) custom-call(f32[104,384]{1,0:T(8,128)} %prefix.1.rows), custom_call_target="tpu_custom_call" | custom-call | tf_op jit(solution)/shard_map/finish/pallas_call | solution.py:782

commit v2 on v1

--- a/solution.py
+++ b/solution.py
@@ -51,12 +51,13 @@
 
 
 class PlaneGather:
-    def __init__(self, unit, rows, core, first, second, to_first, to_second, partner, send, recv, base, sent, straight):
+    def __init__(self, unit, rows, core, first, second, to_first, to_second, partner, send, recv, base, sent, straight, sharing=True):
         self.unit, self.rows, self.core = unit, rows, core
         self.f = [turn(first, d) for d in (0, -1, 1, 2)]
         self.s = [turn(second, d) for d in (0, -1, 1, 2)]
         self.to_first, self.to_second, self.partner = to_first, to_second, partner
         self.send, self.recv, self.base, self.sent, self.straight = send, recv, base, sent, straight
+        self.sharing = sharing
 
     def at(self, kf, ks, half=None, core=None):
         ref = self.unit(self.core if core is None else core, self.f[kf], self.s[ks])
@@ -95,6 +96,8 @@
         self.start(2, source, self.at(0, 0), self.to_first[2])
 
     def share(self, kf, ks, source=None):
+        if not self.sharing:
+            return
         slot = self.at(kf, ks)
         self.start(20 + 4 * ks + kf, slot if source is None else source, slot, self.partner)
 
@@ -139,11 +142,11 @@
 
 def kernel(
     mixing, retention, forcing, observations, model_noise, obs_noise, gain, obs_t, prior_mean, prior_factor,
-    out,
-    ga, gb, cg, ea, eb, ret4, forc4, obs4, noise4, ret8, forc16, obs16, noise8, on_v, gain_v, gain_h, gain_l,
+    means, covariances,
+    ga, gb, gx, cg, ea, eb, ret4, forc4, obs4, noise4, ret8, forc16, obs16, noise8, on_v, gain_v, gain_h, gain_l,
     obs_v, pm_v, pf_v, ct_h, ct_l, fix_h, fix_l, p_h, p_l, b_h, b_l, off8, wc, gc, wf, gf, stage,
     near_mean, t1_h, t1_l, n1_h, n1_l, t2_h, t2_l, n2_h, n2_l, w0_s, v1_s, v2_s, xs,
-    send1, recv1, send3, recv3, send_c, recv_c, send_g, recv_g, send_s, recv_s, send_y, recv_y, send_m, recv_m, local,
+    send1, recv1, send3, recv3, send_c, recv_c, send_g, recv_g, send_s, recv_s, send_y, recv_y, send_m, recv_m, send_b, recv_b, local,
 ):
     y, z, x, c = (lax.axis_index(name) for name in ("y", "z", "x", "c"))
     partner = (y, z, x, 1 - c)
@@ -203,9 +206,9 @@
 
     pl.semaphore_wait(barrier, len(friends))
 
-    first = PlaneGather(lambda core, f, s: ga.at[core, s, f], W, c, x, z, x_to, z_to, partner, send1, recv1, 0, sent, STRAIGHT1)
+    first = PlaneGather(lambda core, f, s: ga.at[core, s, f], W, c, x, z, x_to, z_to, partner, send1, recv1, 0, sent, STRAIGHT1, False)
     other = PlaneGather(
-        lambda core, f, s: gb.at[core, s, f], W, c, z, x, z_to, x_to, partner, send1, recv1, PER_CLASS, sent, STRAIGHT1
+        lambda core, f, s: gb.at[core, s, f], W, c, z, x, z_to, x_to, partner, send1, recv1, PER_CLASS, sent, STRAIGHT1, False
     )
 
     def gain_copy(index, slot, device):
@@ -284,6 +287,8 @@
     def drain():
         for copy in sent:
             copy.wait_send()
+        for index in range(8):
+            swap(index, c).wait_send()
 
         @pl.when(c == 0)
         def _():
@@ -361,69 +366,92 @@
     offsets = product(forc16[...], ct_h[...], ct_l[...]) + product(obs16[...], gain_h[...], gain_l[...], True)
     off8[...] = offsets[:8]
 
-    row_id = lax.broadcasted_iota(jnp.int32, (N, N), 0)
-    col_id = lax.broadcasted_iota(jnp.int32, (N, N), 1)
+    def swap(index, core):
+        slot = gx.at[core, index]
+        return pltpu.make_async_remote_copy(
+            src_ref=slot,
+            dst_ref=slot,
+            send_sem=send_b.at[index],
+            recv_sem=recv_b.at[index],
+            device_id=partner,
+            device_id_type=MESH,
+        )
+
+    def put_first(ks, core, value):
+        high, low = split(value)
+        for spot in range(4):
+            target = pl.ds(pl.multiple_of(spot * 96 + core * W, 16), W)
+            b_h[2 * first.s[ks], target, :] = high[W * spot : W * (spot + 1)]
+            b_l[2 * first.s[ks], target, :] = low[W * spot : W * (spot + 1)]
+
+    def put_other(ks, core, value):
+        high, low = split(value)
+        target = pl.ds(pl.multiple_of(other.s[ks] * 96 + core * W, 16), W)
+        for spot in range(4):
+            b_h[2 * spot + 1, target, :] = high[W * spot : W * (spot + 1)]
+            b_l[2 * spot + 1, target, :] = low[W * spot : W * (spot + 1)]
+
+    def kept(row, offset):
+        return jnp.where(rows_of + offset == cols_of, ret8[pl.ds(row, 1), :], 0.0)
 
     def step_first(ks):
         place = first.s[ks]
-        raw = jnp.concatenate([ga[core, place, spot] for spot in range(4) for core in range(2)], 0)
-        raw = raw + jnp.where(row_id == col_id, ret8[pl.ds(2 * place, 1), :], 0.0)
-        put_split(b_h, b_l, 2 * place, product(raw, ct_h[...], ct_l[...]))
+        raw = [ga[c, place, spot] + kept(2 * place, spot * 96 + c * W) for spot in range(4)]
+        value = product(jnp.concatenate(raw, 0), ct_h[...], ct_l[...])
+        gx[c, ks] = value
+        put_first(ks, c, value)
+        swap(ks, c).start()
 
     def step_other(ks):
         place = other.s[ks]
-        raw = jnp.concatenate(
-            [
-                gb[core, place, spot]
-                + jnp.where(
-                    rows_of + (place * 96 + core * W) == cols_of, ret8[pl.ds(2 * spot + 1, 1), :], 0.0
-                )
-                for spot in range(4)
-                for core in range(2)
-            ],
-            0,
-        )
-        high, low = split(product(raw, ct_h[...], ct_l[...]))
-        target = pl.ds(pl.multiple_of(place * 96, 32), 96)
-        for spot in range(4):
-            b_h[2 * spot + 1, target, :] = high[96 * spot : 96 * (spot + 1)]
-            b_l[2 * spot + 1, target, :] = low[96 * spot : 96 * (spot + 1)]
+        raw = [gb[c, place, spot] + kept(2 * spot + 1, place * 96 + c * W) for spot in range(4)]
+        value = product(jnp.concatenate(raw, 0), ct_h[...], ct_l[...])
+        gx[c, 4 + ks] = value
+        put_other(ks, c, value)
+        swap(4 + ks, c).start()
+
+    def take_first(ks):
+        swap(ks, 1 - c).wait_recv()
+        put_first(ks, 1 - c, gx[1 - c, ks])
+
+    def take_other(ks):
+        swap(4 + ks, 1 - c).wait_recv()
+        put_other(ks, 1 - c, gx[1 - c, 4 + ks])
 
     def ready(gather, ks):
         for kf in range(4):
             gather.shared(kf, ks)
 
-    ready(first, 0)
     step_first(0)
     first.second_near(1)
     other.second_near(1)
-    ready(other, 0)
     step_other(0)
     first.second_near(2)
     other.second_near(2)
-
+    take_first(0)
     first.second_near(3)
     other.second_near(3)
-    ready(first, 1)
     step_first(1)
     first.second_far(0)
     other.second_far(0)
-    ready(first, 2)
     step_first(2)
     first.second_far(1)
     other.second_far(1)
-    ready(other, 1)
     step_other(1)
     first.second_far(2)
     other.second_far(2)
-    ready(other, 2)
     step_other(2)
+    take_other(0)
+    take_first(1)
+    take_first(2)
+    take_other(1)
     first.second_far(3)
     other.second_far(3)
-    ready(first, 3)
     step_first(3)
-    ready(other, 3)
     step_other(3)
+    take_other(2)
+    take_first(3)
+    take_other(3)
 
     row32 = lax.broadcasted_iota(jnp.int32, (32, N), 0)
     col32 = lax.broadcasted_iota(jnp.int32, (32, N), 1)
@@ -686,18 +714,23 @@
         value = product(xs[...], b_h[j], b_l[j])
         xs[...] = value + jnp.concatenate([gf[j], mean_rows(off8[pl.ds(j, 1), :])], 0)
 
-    out[pl.ds(0, W), :] = xs[pl.ds(0, W), :]
-    out[pl.ds(96, 1), :] = xs[pl.ds(96, 1), :]
+    covariances[0] = xs[pl.ds(0, W), :]
+    means[pl.ds(0, 1), :] = xs[pl.ds(96, 1), :]
     value = product(xs[pl.ds(W, 64), :], b_h[last], b_l[last])
-    out[pl.ds(W, W), :] = value[:W] + gf[last, pl.ds(W, W), :]
-    out[pl.ds(97, 1), :] = value[W : W + 1] + off8[pl.ds(last, 1), :]
+    covariances[1] = value[:W] + gf[last, pl.ds(W, W), :]
+    means[pl.ds(1, 1), :] = value[W : W + 1] + off8[pl.ds(last, 1), :]
     drain()
 
 
-def finish(rows, means, covariances):
-    covariances[0] = rows[pl.ds(0, W), :]
-    covariances[1] = rows[pl.ds(W, W), :]
-    means[...] = rows[pl.ds(96, 2), :]
+def finish(near_means, near_covariances, means, covariances, done):
+    copies = [
+        pltpu.make_async_copy(near_means, means, done.at[0]),
+        pltpu.make_async_copy(near_covariances, covariances, done.at[1]),
+    ]
+    for copy in copies:
+        copy.start()
+    for copy in copies:
+        copy.wait()
 
 
 def vmem(shape, dtype=F32):
@@ -711,14 +744,15 @@
 def per_device(mixing, retention, forcing, observations, model_noise, obs_noise, gain, obs_t, prior_mean, prior_factor):
     dma = pltpu.SemaphoreType.DMA
     square = (N, N)
-    rows = pl.pallas_call(
+    near = pl.pallas_call(
         kernel,
-        out_shape=jax.ShapeDtypeStruct((104, N), F32),
-        in_specs=[pl.BlockSpec(memory_space=pl.ANY)] * 10,
-        out_specs=pl.BlockSpec(memory_space=pltpu.VMEM),
+        out_shape=(pltpu.VMEM((2, N), F32), pltpu.VMEM((2, W, N), F32)),
+        in_specs=[pl.BlockSpec(memory_space=pltpu.HBM)] * 10,
+        out_specs=(pl.BlockSpec(memory_space=pltpu.VMEM),) * 2,
         scratch_shapes=[
             vmem((2, 4, 4, W, N)),
             vmem((2, 4, 4, W, N)),
+            vmem((2, 8, 4 * W, N)),
             vmem((2, 4, W, N)),
             vmem((2, 4, 4, CR, N)),
             vmem((2, 4, 4, CR, N)),
@@ -769,10 +803,12 @@
             dma((7,)),
             dma((3,)),
             dma((3,)),
+            dma((8,)),
+            dma((8,)),
             dma((11,)),
         ],
         compiler_params=pltpu.CompilerParams(
-            collective_id=0, has_side_effects=True, vmem_limit_bytes=67043328
+            collective_id=0, has_side_effects=True, vmem_limit_bytes=60 * 1024 * 1024
         ),
         name="prefix",
     )(
@@ -782,10 +818,12 @@
     return pl.pallas_call(
         finish,
         out_shape=(jax.ShapeDtypeStruct((2, N), F32), jax.ShapeDtypeStruct((2, W, N), F32)),
-        in_specs=[pl.BlockSpec(memory_space=pltpu.VMEM)],
-        out_specs=(pl.BlockSpec(memory_space=pltpu.VMEM),) * 2,
+        in_specs=[pl.BlockSpec(memory_space=pltpu.VMEM)] * 2,
+        out_specs=(pl.BlockSpec(memory_space=pltpu.HBM),) * 2,
+        scratch_shapes=[pltpu.SemaphoreType.DMA((2,))],
+        compiler_params=pltpu.CompilerParams(vmem_limit_bytes=1024 * 1024),
         name="finish",
-    )(rows)
+    )(*near)
 
 
 def solution(mesh):

time: 57 us -> 54.9 us (0.963)
  Pallas kernels: 56.2 us -> 54 us
    pallas_call x1, Pallas kernels: 54.7 us -> 53.3 us  [per_device(): pl.pallas_call(kernel, out_shape=(pltpu.VMEM((2, N), F32), pltpu.VMEM((2,...]
    pallas_call x1, Pallas kernels: 1.59 us -> 0.68 us  [per_device(): pl.pallas_call(finish, out_shape=(jax.ShapeDtypeStruct((2, N), F32), jax....]
where the time goes in v2:
time: 54.9 us; the launch traced here: 54.8 us
  Pallas kernels  54 us (98%)
  between operations  0.8 us (1%)
    pallas_call x1, Pallas kernels, per_device(): pl.pallas_call(kernel, out_shape=(pltpu.VMEM((2, N), F32), pltpu.VMEM((2,...  53.3 us

profile of v2, /device:TPU:120, one launch (start us, length us, event | category | flops | bytes accessed | tf_op | source)
XLA Modules:
  0.0 54.8 jit_solution(16474404504747512278)
XLA Ops:
  0.6 53.3 %prefix.1 = (f32[2,384]{1,0:T(2,128)S(1)}, f32[2,48,384]{2,1,0:T(8,128)S(1)}) custom-call(f32[2,48,384]{2,1,0:T(8,128)} %mixing.1, f32[2,384]{1,0:T(2,128)} %retention.1, f32[2,384]{1,0:T(2,128)} %forcing.1, f32[2,1024]{1,0:T(2,128)} %observations.1, f32[2,384]{1,0:T(2,128)} %model_noise.1, f32[1,1024]{1,0:T(1,128)} %bitcast.1, f32[384,1024]{1,0:T(8,128)} %gain.1, ...), custom_call_target="tpu_custom_call" | custom-call | tf_op jit(solution)/shard_map/prefix/pallas_call | solution.py:747
  53.9 0.7 %finish.1 = (f32[2,384]{1,0:T(2,128)}, f32[2,48,384]{2,1,0:T(8,128)}) custom-call(f32[2,384]{1,0:T(2,128)S(1)} %get-tuple-element.4.near_means, f32[2,48,384]{2,1,0:T(8,128)S(1)} %get-tuple-element.5.near_covariances), custom_call_target="tpu_custom_call" | custom-call | tf_op jit(solution)/shard_map/finish/pallas_call | solution.py:818

commit v3 on v2

--- a/solution.py
+++ b/solution.py
@@ -145,7 +145,7 @@
     means, covariances,
     ga, gb, gx, cg, ea, eb, ret4, forc4, obs4, noise4, ret8, forc16, obs16, noise8, on_v, gain_v, gain_h, gain_l,
     obs_v, pm_v, pf_v, ct_h, ct_l, fix_h, fix_l, p_h, p_l, b_h, b_l, off8, wc, gc, wf, gf, stage,
-    near_mean, t1_h, t1_l, n1_h, n1_l, t2_h, t2_l, n2_h, n2_l, w0_s, v1_s, v2_s, xs,
+    near_mean, t1_h, t1_l, n1_h, n1_l, t2_h, t2_l, n2_h, n2_l, w0_s, v1_s, v2_s, xs, nz, ph_f, ph_h, ph_l,
     send1, recv1, send3, recv3, send_c, recv_c, send_g, recv_g, send_s, recv_s, send_y, recv_y, send_m, recv_m, send_b, recv_b, local,
 ):
     y, z, x, c = (lax.axis_index(name) for name in ("y", "z", "x", "c"))
@@ -289,6 +289,7 @@
             copy.wait_send()
         for index in range(8):
             swap(index, c).wait_send()
+        swap_phi(c).wait_send()
 
         @pl.when(c == 0)
         def _():
@@ -549,6 +550,28 @@
         stage[2, :, pl.ds(128, 128)] = jnp.where(low, two, jnp.where(high, one, three))
         ships(False, lambda copy: copy.start())
 
+    last = 2 * z + 1
+    wf[last, pl.ds(W, W), :] = eye_rows
+    behind = product(eye_rows, b_h[last], b_l[last], True)
+    w0_s[pl.ds(0, W), :] = eye_rows
+    w0_s[pl.ds(W, W), :] = behind
+
+    @pl.loop(0, 2 * z + 1)
+    def _(i):
+        j = 2 * z - i
+        rows = w0_s[...]
+        wf[j] = rows
+        w0_s[...] = product(rows, b_h[j], b_l[j], True)
+
+    def noise_rows(part):
+        span = pl.ds(4 * part, 4)
+        rows = wf[span].reshape(N, N)
+        wide = product(rows, ct_h[...], ct_l[...], True).reshape(4, 96, N)
+        wide = wide * noise8[pl.ds(4 * part, 4), :].reshape(4, 1, N)
+        value = product(wide.reshape(N, N), ct_h[...], ct_l[...]) + product(rows, fix_h[...], fix_l[...])
+        gf[span] = value.reshape(4, 96, N)
+
+
     @pl.when((c == 0) & (y >= 2))
     def _():
         ship(0, mine_a, mine_a, 2, partner).wait_recv()
@@ -589,59 +612,70 @@
             ship(0, near_mean.at[plane], near_mean.at[plane], 4 + plane, partner).wait_recv()
             pass_mean(plane).start()
 
-    last = 2 * z + 1
-    wf[last, pl.ds(W, W), :] = eye_rows
-    behind = product(eye_rows, b_h[last], b_l[last], True)
-    w0_s[pl.ds(0, W), :] = eye_rows
-    w0_s[pl.ds(W, W), :] = behind
+    own_half = pl.ds(pl.multiple_of(c * 192, 64), 192)
+    ph_f[c] = b_h[0, own_half, :].astype(F32) + b_l[0, own_half, :].astype(F32)
+
+    @pl.loop(1, 2 * z + 1)
+    def _(j):
+        ph_f[c] = product(ph_f[c], b_h[j], b_l[j])
+
+    def swap_phi(core):
+        slot = ph_f.at[core]
+        return pltpu.make_async_remote_copy(
+            src_ref=slot,
+            dst_ref=slot,
+            send_sem=send_b.at[8],
+            recv_sem=recv_b.at[8],
+            device_id=partner,
+            device_id_type=MESH,
+        )
 
     third.first_near()
     fourth.first_near()
     third.first_far()
     fourth.first_far()
-
-    @pl.loop(0, 2 * z + 1)
-    def _(i):
-        j = 2 * z - i
-        rows = w0_s[...]
-        wf[j] = rows
-        w0_s[...] = product(rows, b_h[j], b_l[j], True)
-
-    def noise_rows(part):
-        span = pl.ds(4 * part, 4)
-        rows = wf[span].reshape(N, N)
-        wide = product(rows, ct_h[...], ct_l[...], True).reshape(4, 96, N)
-        wide = wide * noise8[pl.ds(4 * part, 4), :].reshape(4, 1, N)
-        value = product(wide.reshape(N, N), ct_h[...], ct_l[...]) + product(rows, fix_h[...], fix_l[...])
-        gf[span] = value.reshape(4, 96, N)
+    swap_phi(c).start()
+    noise_rows(0)
 
     third.second_near(0)
     fourth.second_near(0)
-    noise_rows(0)
+
+    @pl.when(z >= 2)
+    def _():
+        noise_rows(1)
+
     for kf in (1, 2):
         third.second_near(kf)
         fourth.second_near(kf)
 
-    @pl.when(z >= 2)
-    def _():
-        noise_rows(1)
+    row16 = lax.broadcasted_iota(jnp.int32, (16, N), 0)
+
+    def mean_rows(row):
+        return jnp.where(row16 == 0, row, 0.0)
+
+    def fresh(j):
+        return jnp.concatenate([gf[j], mean_rows(off8[pl.ds(j, 1), :])], 0)
+
+    nz[...] = fresh(0)
+
+    @pl.loop(1, z + 1)
+    def _(j):
+        nz[...] = product(nz[...], b_h[j], b_l[j]) + fresh(j)
 
     third.second_near(3)
     fourth.second_near(3)
-    for kf in range(4):
-        third.second_far(kf)
-        fourth.second_far(kf)
-    for ks in range(4):
-        ready(third, ks)
-        ready(fourth, ks)
+
+    @pl.loop(z + 1, 2 * z + 1)
+    def _(j):
+        nz[...] = product(nz[...], b_h[j], b_l[j]) + fresh(j)
+
+    swap_phi(1 - c).wait_recv()
+    for core in range(2):
+        high, low = split(ph_f[core])
+        ph_h[pl.ds(192 * core, 192), :] = high
+        ph_l[pl.ds(192 * core, 192), :] = low
 
     spots = [(a, b) for a in range(4) for b in range(4)]
-
-    for plane in range(3):
-
-        @pl.when((c == 0) & (y > plane))
-        def _():
-            pass_mean(plane).wait_recv()
 
     def symmetric(own, after):
         d0, d1, d2 = (own[128 * b : 128 * (b + 1)] for b in range(3))
@@ -658,34 +692,61 @@
     def from_b(a, b):
         return eb[1, b, a]
 
+    def ready_all():
+        for ks in range(4):
+            ready(third, ks)
+            ready(fourth, ks)
+
+    def prepare_steps():
+        @pl.when(y == 3)
+        def _():
+            put_split(t2_h, t2_l, ..., jnp.concatenate([eb[0, b, a] for a, b in spots], 0))
+            v2_s[...] = product(w0_s[...], t2_h[...], t2_l[...])
+
+        @pl.when(y != 3)
+        def _():
+            v2_s[...] = w0_s[...]
+
+        @pl.when(y >= 2)
+        def _():
+            put_split(t1_h, t1_l, ..., jnp.concatenate([ea[0, a, b] for a, b in spots], 0))
+            v1_s[...] = product(v2_s[...], t1_h[...], t1_l[...])
+
+        @pl.when(y < 2)
+        def _():
+            v1_s[...] = v2_s[...]
+
+    for kf in range(4):
+        third.second_far(kf)
+        fourth.second_far(kf)
+
+    @pl.when(c == 0)
+    def _():
+        prepare_steps()
+        ready_all()
+
+    @pl.when(c == 1)
+    def _():
+        ready_all()
+        prepare_steps()
+
+    for plane in range(3):
+
+        @pl.when((c == 0) & (y > plane))
+        def _():
+            pass_mean(plane).wait_recv()
+
+    @pl.when(y >= 1)
+    def _():
+        put_split(p_h, p_l, ..., symmetric(columns(from_a, 2), columns(from_b, 2)))
+
+    @pl.when(y >= 2)
+    def _():
+        put_split(n1_h, n1_l, ..., symmetric(columns(from_a, 0), columns(from_a, 1)))
+
     @pl.when(y == 3)
     def _():
-        put_split(t2_h, t2_l, ..., jnp.concatenate([eb[0, b, a] for a, b in spots], 0))
         put_split(n2_h, n2_l, ..., symmetric(columns(from_b, 0), columns(from_b, 1)))
-        v2_s[...] = product(w0_s[...], t2_h[...], t2_l[...])
-
-    @pl.when(y != 3)
-    def _():
-        v2_s[...] = w0_s[...]
-
-    @pl.when(y >= 2)
-    def _():
-        put_split(t1_h, t1_l, ..., jnp.concatenate([ea[0, a, b] for a, b in spots], 0))
-        put_split(n1_h, n1_l, ..., symmetric(columns(from_a, 0), columns(from_a, 1)))
-        v1_s[...] = product(v2_s[...], t1_h[...], t1_l[...])
-
-    @pl.when(y < 2)
-    def _():
-        v1_s[...] = v2_s[...]
-
-    @pl.when(y >= 1)
-    def _():
-        put_split(p_h, p_l, ..., symmetric(columns(from_a, 2), columns(from_b, 2)))
-
-    row16 = lax.broadcasted_iota(jnp.int32, (16, N), 0)
-
-    def mean_rows(row):
-        return jnp.where(row16 == 0, row, 0.0)
 
     xs[pl.ds(0, 96), :] = product(v1_s[...], p_h[...], p_l[...])
 
@@ -709,10 +770,7 @@
         added = product(w0_s[...], n2_h[...], n2_l[...])
         xs[...] = value + jnp.concatenate([added, mean_rows(near_mean[2, pl.ds(0, 1), :])], 0)
 
-    @pl.loop(0, 2 * z + 1)
-    def _(j):
-        value = product(xs[...], b_h[j], b_l[j])
-        xs[...] = value + jnp.concatenate([gf[j], mean_rows(off8[pl.ds(j, 1), :])], 0)
+    xs[...] = product(xs[...], ph_h[...], ph_l[...]) + nz[...]
 
     covariances[0] = xs[pl.ds(0, W), :]
     means[pl.ds(0, 1), :] = xs[pl.ds(96, 1), :]
@@ -789,6 +847,9 @@
             vmem((96, N)),
             vmem((96, N)),
             vmem((112, N)),
+            vmem((112, N)),
+            vmem((2, 192, N)),
+            *pair(square),
             dma((2 * PER_CLASS,)),
             dma((2 * PER_CLASS,)),
             dma((2 * PER_CLASS,)),
@@ -803,8 +864,8 @@
             dma((7,)),
             dma((3,)),
             dma((3,)),
-            dma((8,)),
-            dma((8,)),
+            dma((9,)),
+            dma((9,)),
             dma((11,)),
         ],
         compiler_params=pltpu.CompilerParams(

time: 54.9 us -> 53.3 us (0.971)
  the two profiles are of different devices: /device:TPU:120 before, /device:TPU:25 now
where the time goes in v3:
time: 53.3 us; the launch traced here: 53.2 us
  Pallas kernels  52.4 us (98%)
  between operations  0.8 us (2%)
    pallas_call x1, Pallas kernels, per_device(): pl.pallas_call(kernel, out_shape=(pltpu.VMEM((2, N), F32), pltpu.VMEM((2,...  51.7 us

profile of v3, /device:TPU:25, one launch (start us, length us, event | category | flops | bytes accessed | tf_op | source)
XLA Modules:
  0.0 53.2 jit_solution(7896338234981022592)
XLA Ops:
  0.6 51.7 %prefix.1 = (f32[2,384]{1,0:T(2,128)S(1)}, f32[2,48,384]{2,1,0:T(8,128)S(1)}) custom-call(f32[2,48,384]{2,1,0:T(8,128)} %mixing.1, f32[2,384]{1,0:T(2,128)} %retention.1, f32[2,384]{1,0:T(2,128)} %forcing.1, f32[2,1024]{1,0:T(2,128)} %observations.1, f32[2,384]{1,0:T(2,128)} %model_noise.1, f32[1,1024]{1,0:T(1,128)} %bitcast.1, f32[384,1024]{1,0:T(8,128)} %gain.1, ...), custom_call_target="tpu_custom_call" | custom-call | tf_op jit(solution)/shard_map/prefix/pallas_call | solution.py:805
  52.3 0.7 %finish.1 = (f32[2,384]{1,0:T(2,128)}, f32[2,48,384]{2,1,0:T(8,128)}) custom-call(f32[2,384]{1,0:T(2,128)S(1)} %get-tuple-element.4.near_means, f32[2,48,384]{2,1,0:T(8,128)S(1)} %get-tuple-element.5.near_covariances), custom_call_target="tpu_custom_call" | custom-call | tf_op jit(solution)/shard_map/finish/pallas_call | solution.py:879

commit v4 on v3

--- a/solution.py
+++ b/solution.py
@@ -736,39 +736,33 @@
         def _():
             pass_mean(plane).wait_recv()
 
-    @pl.when(y >= 1)
-    def _():
-        put_split(p_h, p_l, ..., symmetric(columns(from_a, 2), columns(from_b, 2)))
+    def covariance_before():
+        return split(symmetric(columns(from_a, 2), columns(from_b, 2)))
+
+    def mean_of(plane):
+        return mean_rows(near_mean[plane, pl.ds(0, 1), :])
+
+    def joined(rows, row):
+        return jnp.concatenate([rows, row], 0)
+
+    @pl.when(y == 0)
+    def _():
+        xs[...] = joined(product(v1_s[...], p_h[...], p_l[...]), mean_rows(pm_v[...].reshape(1, N)))
+
+    @pl.when(y == 1)
+    def _():
+        xs[...] = joined(product(v1_s[...], *covariance_before()), mean_of(0))
 
     @pl.when(y >= 2)
     def _():
-        put_split(n1_h, n1_l, ..., symmetric(columns(from_a, 0), columns(from_a, 1)))
-
-    @pl.when(y == 3)
-    def _():
-        put_split(n2_h, n2_l, ..., symmetric(columns(from_b, 0), columns(from_b, 1)))
-
-    xs[pl.ds(0, 96), :] = product(v1_s[...], p_h[...], p_l[...])
-
-    @pl.when(y == 0)
-    def _():
-        xs[pl.ds(96, 16), :] = mean_rows(pm_v[...].reshape(1, N))
-
-    @pl.when(y >= 1)
-    def _():
-        xs[pl.ds(96, 16), :] = mean_rows(near_mean[0, pl.ds(0, 1), :])
-
-    @pl.when(y >= 2)
-    def _():
-        value = product(xs[...], t1_h[...], t1_l[...], True)
-        added = product(v2_s[...], n1_h[...], n1_l[...])
-        xs[...] = value + jnp.concatenate([added, mean_rows(near_mean[1, pl.ds(0, 1), :])], 0)
+        value = joined(product(v1_s[...], *covariance_before()), mean_of(0))
+        added = product(v2_s[...], *split(symmetric(columns(from_a, 0), columns(from_a, 1))))
+        xs[...] = product(value, t1_h[...], t1_l[...], True) + joined(added, mean_of(1))
 
     @pl.when(y >= 3)
     def _():
-        value = product(xs[...], t2_h[...], t2_l[...], True)
-        added = product(w0_s[...], n2_h[...], n2_l[...])
-        xs[...] = value + jnp.concatenate([added, mean_rows(near_mean[2, pl.ds(0, 1), :])], 0)
+        added = product(w0_s[...], *split(symmetric(columns(from_b, 0), columns(from_b, 1))))
+        xs[...] = product(xs[...], t2_h[...], t2_l[...], True) + joined(added, mean_of(2))
 
     xs[...] = product(xs[...], ph_h[...], ph_l[...]) + nz[...]
 

time: 53.3 us -> 53 us (level)
  no operation moved by 1% of the time
where the time goes in v4:
time: 53 us; the launch traced here: 52.9 us
  Pallas kernels  52.1 us (98%)
  between operations  0.8 us (2%)
    pallas_call x1, Pallas kernels, per_device(): pl.pallas_call(kernel, out_shape=(pltpu.VMEM((2, N), F32), pltpu.VMEM((2,...  51.4 us

profile of v4, /device:TPU:25, one launch (start us, length us, event | category | flops | bytes accessed | tf_op | source)
XLA Modules:
  0.0 52.9 jit_solution(9833493133480504218)
XLA Ops:
  0.6 51.4 %prefix.1 = (f32[2,384]{1,0:T(2,128)S(1)}, f32[2,48,384]{2,1,0:T(8,128)S(1)}) custom-call(f32[2,48,384]{2,1,0:T(8,128)} %mixing.1, f32[2,384]{1,0:T(2,128)} %retention.1, f32[2,384]{1,0:T(2,128)} %forcing.1, f32[2,1024]{1,0:T(2,128)} %observations.1, f32[2,384]{1,0:T(2,128)} %model_noise.1, f32[1,1024]{1,0:T(1,128)} %bitcast.1, f32[384,1024]{1,0:T(8,128)} %gain.1, ...), custom_call_target="tpu_custom_call" | custom-call | tf_op jit(solution)/shard_map/prefix/pallas_call | solution.py:799
  52.0 0.7 %finish.1 = (f32[2,384]{1,0:T(2,128)}, f32[2,48,384]{2,1,0:T(8,128)}) custom-call(f32[2,384]{1,0:T(2,128)S(1)} %get-tuple-element.4.near_means, f32[2,48,384]{2,1,0:T(8,128)S(1)} %get-tuple-element.5.near_covariances), custom_call_target="tpu_custom_call" | custom-call | tf_op jit(solution)/shard_map/finish/pallas_call | solution.py:873

commit v5 on v4

--- a/solution.py
+++ b/solution.py
@@ -447,8 +447,8 @@
     take_first(2)
     take_other(1)
     first.second_far(3)
+    step_first(3)
     other.second_far(3)
-    step_first(3)
     step_other(3)
     take_other(2)
     take_first(3)

time: 53 us -> 53.5 us (level)
  no operation moved by 1% of the time
where the time goes in v5:
time: 53.5 us; the launch traced here: 53.3 us
  Pallas kernels  52.5 us (98%)
  between operations  0.8 us (1%)
    pallas_call x1, Pallas kernels, per_device(): pl.pallas_call(kernel, out_shape=(pltpu.VMEM((2, N), F32), pltpu.VMEM((2,...  51.9 us

profile of v5, /device:TPU:25, one launch (start us, length us, event | category | flops | bytes accessed | tf_op | source)
XLA Modules:
  0.0 53.3 jit_solution(13267277892278509670)
XLA Ops:
  0.6 51.9 %prefix.1 = (f32[2,384]{1,0:T(2,128)S(1)}, f32[2,48,384]{2,1,0:T(8,128)S(1)}) custom-call(f32[2,48,384]{2,1,0:T(8,128)} %mixing.1, f32[2,384]{1,0:T(2,128)} %retention.1, f32[2,384]{1,0:T(2,128)} %forcing.1, f32[2,1024]{1,0:T(2,128)} %observations.1, f32[2,384]{1,0:T(2,128)} %model_noise.1, f32[1,1024]{1,0:T(1,128)} %bitcast.1, f32[384,1024]{1,0:T(8,128)} %gain.1, ...), custom_call_target="tpu_custom_call" | custom-call | tf_op jit(solution)/shard_map/prefix/pallas_call | solution.py:799
  52.5 0.7 %finish.1 = (f32[2,384]{1,0:T(2,128)}, f32[2,48,384]{2,1,0:T(8,128)}) custom-call(f32[2,384]{1,0:T(2,128)S(1)} %get-tuple-element.4.near_means, f32[2,48,384]{2,1,0:T(8,128)S(1)} %get-tuple-element.5.near_covariances), custom_call_target="tpu_custom_call" | custom-call | tf_op jit(solution)/shard_map/finish/pallas_call | solution.py:873
